TPU v7x, 256 devices: a whole 4x4x8 slice. The times are simulated.
256 devices in a mesh: inst: 8 (over y_hi, x), space: 32 (over z, y_lo, core).
Axes of the slice: x: 4, y: 4 (y_hi: 2, y_lo: 2; y = y_hi * 2 + y_lo), z: 8, core: 2. Of those that a mesh axis runs over, the one named last changes fastest.
Arguments:
- psi_start: float32 [5, 8, 256, 1024], P(None, 'inst', 'space'), may hold values from -6 to 6
- density: float32 [8, 256, 1024], P('inst', 'space'), may hold values from 0.8 to 1.25
- velocity: float32 [3, 8, 256, 1024], P(None, 'inst', 'space'), may hold values from -0.6 to 0.6
- pressure: float32 [8, 256, 1024], P('inst', 'space'), may hold values from 0.5 to 1
- obs_pos: float32 [3, 512], P(None, 'space'), may hold values from -16 to 16, as said below
- obs_weight: float32 [2, 512], P(None, 'space'), may hold values from -0.6 to 0.6
- obs_harmonic: int32 [512], P('space'), may hold values from 1 to 3
- panel_pos: float32 [3, 65536], replicated, may hold values from -1 to 1
- panel_normal: float32 [3, 65536], P(None, 'space'), may hold values from -5 to 5
- panel_cell: int32 [65536], P('space'), may hold values from 0 to 8191
- plane_nbr: int32 [4, 1024], replicated, may hold values from 0 to 1023
Outputs:
- adjoint: float32 [5, 8, 256, 1024], P(None, 'inst', 'space')
Inputs may be any that keep to these rules, and one draw needn't show every extreme that they name: `obs_pos`: observers lie between 8 and 16 from the anchor, outside the panels' cube. panel_cell[q] is an index into the 8 x 1024 cells of the slot's owner, layer panel_cell[q] // 1024.
All inputs are finite; a program needn't handle non-finite values.
Results may differ from a plain program's by a relative error of at most 0.0001.
Values sent between devices are 32-bit elements; how exact they have to be, the bound alone decides.
A program may use at most 64 MiB of HBM per device.

v0:
```python
import math
import jax
import jax.numpy as jnp
from jax import lax
from jax.sharding import PartitionSpec as P

ITERS = 3
GAMMA = 1.4
KWAVE = 0.7
RADIUS = 10.0
TAU = 0.05
DISSIP = 0.25
OMEGA = 1.5
VISCO = 0.5


def padded_2(cells, sides, width):
    for axis, dim in sides:
        count = lax.axis_size(axis)
        head = lax.slice_in_dim(cells, 0, width, axis=dim)
        tail = lax.slice_in_dim(cells, cells.shape[dim] - width, cells.shape[dim], axis=dim)
        cells = jnp.concatenate(
            [
                lax.ppermute(tail, axis, [(i, (i + 1) % count) for i in range(count)]),
                cells,
                lax.ppermute(head, axis, [((i + 1) % count, i) for i in range(count)]),
            ],
            axis=dim,
        )
    return cells


def panel_block(observers, panels, time_now):
    delta = panels[:, None, :] - observers[:3, :, None]
    dist2 = jnp.sum(delta * delta, axis=0)
    dist = jnp.sqrt(dist2)
    harm = observers[5][:, None]
    phase = harm * (time_now - KWAVE * dist)
    amp = (
        (observers[3][:, None] * jnp.cos(phase) + observers[4][:, None] * jnp.sin(phase))
        * (RADIUS * RADIUS)
        / (dist2 * dist)
    )
    return jnp.sum(amp[None] * delta, axis=1)


def sensitivity(observers, panels, time_now):
    count = panels.shape[1]
    obs_count = observers.shape[1]
    block = math.gcd(count, max(128, 262144 // obs_count))
    split = panels.reshape(3, count // block, block).transpose(1, 0, 2)
    out = lax.map(lambda piece: panel_block(observers, piece, time_now), split)
    return out.transpose(1, 0, 2).reshape(3, count)


def conserved(density, velocity, pressure):
    moment = density[None] * velocity
    energy = pressure / (GAMMA - 1.0) + 0.5 * density * jnp.sum(velocity * velocity, axis=0)
    return jnp.concatenate([density[None], moment, energy[None]], axis=0)


def fluxes(state):
    dens = state[0]
    moment = state[1:4]
    energy = state[4]
    vel = moment / dens
    press = (GAMMA - 1.0) * (energy - 0.5 * jnp.sum(moment * vel, axis=0))
    result = []
    for axis_d in range(3):
        comps = [moment[axis_d]]
        for axis_e in range(3):
            term = moment[axis_e] * vel[axis_d]
            if axis_e == axis_d:
                term = term + press
            comps.append(term)
        comps.append((energy + press) * vel[axis_d])
        result.append(jnp.stack(comps))
    return tuple(result)


def spectral_coeff(offset, count):
    safe = jnp.where(offset == 0, 1.0, offset)
    angle = math.pi * safe / count
    even_odd_flag = 1.0 - 2.0 * jnp.mod(safe, 2.0)
    other = (
        -(OMEGA / 2.0) * even_odd_flag * jnp.cos(angle) / jnp.sin(angle)
        + VISCO * (OMEGA * OMEGA / 2.0) * even_odd_flag / jnp.sin(angle) ** 2
    )
    return jnp.where(offset == 0, VISCO * OMEGA * OMEGA * (count * count + 2.0) / 12.0, other)


def shards(
    psi_start,
    density,
    velocity,
    pressure,
    obs_pos,
    obs_weight,
    obs_harmonic,
    panel_pos,
    panel_normal,
    panel_cell,
    plane_nbr,
):
    inst_count = lax.axis_size("inst")
    inst_id = lax.axis_index("inst")
    space_id = lax.axis_index("space")
    time_now = 2.0 * math.pi * inst_id.astype(jnp.float32) / inst_count
    observers = jnp.concatenate(
        [obs_pos, obs_weight, obs_harmonic[None].astype(jnp.float32)], axis=0
    )
    owned_count = panel_normal.shape[1]
    whole = sensitivity(observers, panel_pos, time_now)
    total = lax.psum(whole, "space")
    sens = lax.dynamic_slice_in_dim(total, space_id * owned_count, owned_count, 1)
    weight = jnp.sum(sens * panel_normal, axis=0)
    layers = psi_start.shape[2]
    plane = psi_start.shape[3]
    wall = jax.ops.segment_sum(weight, panel_cell, num_segments=layers * plane).reshape(
        layers, plane
    )
    dens = density[0]
    vel = velocity[:, 0]
    state = conserved(dens, vel, pressure[0])
    slope = jnp.concatenate(
        [0.5 * jnp.sum(vel * vel, axis=0)[None], -vel, jnp.ones_like(dens)[None]], axis=0
    ) * (GAMMA - 1.0)
    source = slope * wall[None]
    _, pull = jax.vjp(fluxes, state)
    psi = psi_start[:, 0]
    for step in range(ITERS):
        padded = padded_2(psi, (("space", 1),), 1)
        minus_a = padded[:, :-2]
        plus_a = padded[:, 2:]
        plus_y = jnp.take(psi, plane_nbr[0], axis=2)
        minus_y = jnp.take(psi, plane_nbr[1], axis=2)
        plus_z = jnp.take(psi, plane_nbr[2], axis=2)
        minus_z = jnp.take(psi, plane_nbr[3], axis=2)
        middle_point = pull(
            (0.5 * (minus_a - plus_a), 0.5 * (minus_y - plus_y), 0.5 * (minus_z - plus_z))
        )[0]
        spread = 6.0 * psi - (minus_a + plus_a + plus_y + minus_y + plus_z + minus_z)
        every_instant = lax.all_gather(psi[:, None], "inst", axis=1, tiled=True)
        others = jnp.arange(inst_count, dtype=jnp.int32)
        row_entry = spectral_coeff(
            jnp.mod(inst_id - others, inst_count).astype(jnp.float32), float(inst_count)
        )
        spectral_operator = jnp.einsum(
            "c,kcyo->kyo", row_entry, every_instant, precision=lax.Precision.HIGHEST
        )
        psi = psi - TAU * (middle_point + DISSIP * spread + spectral_operator + source)
    return psi[:, None]


def solution(mesh):
    placed = (
        P(None, "inst", "space", None),
        P("inst", "space", None),
        P(None, "inst", "space", None),
        P("inst", "space", None),
        P(None, "space"),
        P(None, "space"),
        P("space"),
        P(),
        P(None, "space"),
        P("space"),
        P(),
    )
    return jax.shard_map(
        shards,
        mesh=mesh,
        in_specs=placed,
        out_specs=P(None, "inst", "space", None),
        check_vma=False,
    )
```

profile of v0, /device:TPU:2, one launch (start us, length us, event | category | flops | bytes accessed | tf_op | source)
XLA Modules:
  0.0 505.2 jit_solution(14409982304165432410)
XLA Ops:
  8.0 38.1 %while.10 = (s32[]{:T(128)}, f32[4,3,16384]{2,1,0:T(4,128)}, f32[2,16]{1,0:T(2,128)}, f32[1,16]{1,0:T(1,128)S(1)}, f32[]{:T(128)}, /*index=5*/f32[4,3,16384]{2,1,0:T(4,128)}, f32[3,16]{1,0:T(4,128)}, s32[]{:T(128)}) while((s32[]{:T(128)}, f32[4,3,16384]{2,1,0:T(4,128)}, f32[2,16]{1,0:T(2,128)}, f32[1,16]{1,0:T(1,128)S(1)}, f32[]{:T(128)}, ...), condition=%wide.region_6.8_spmd, body=%wide.region_3.7_spmd.sunk | while | flops 6766594 | bytes 5637533 | solution.py:52
  8.0 1.0 dynamic-slice_bitcast_fusion.2
  9.1 1.2 fusion.107
  10.3 0.8 slice_bitcast_fusion.3
  11.1 4.3 fusion.108
  15.4 1.5 fusion.109
  16.8 0.8 bitcast_dynamic-update-slice_fusion.2
  17.6 1.0 dynamic-slice_bitcast_fusion.2
  18.6 1.2 fusion.107
  19.8 0.8 slice_bitcast_fusion.3
  20.6 4.3 fusion.108
  24.9 1.5 fusion.109
  27.1 1.0 dynamic-slice_bitcast_fusion.2
  28.1 1.2 fusion.107
  29.3 0.8 slice_bitcast_fusion.3
  30.1 4.3 fusion.108
  34.4 1.5 fusion.109
  36.6 1.0 dynamic-slice_bitcast_fusion.2
  37.6 1.2 fusion.107
  38.9 0.8 slice_bitcast_fusion.3
  39.6 4.3 fusion.108
  43.9 1.5 fusion.109
  46.2 1.0 fusion.102
  47.3 6.4 %collective-permute-start.1 = (f32[5,1,1024]{2,1,0:T(1,128)S(1)}, f32[5,1,1024]{2,1,0:T(1,128)S(1)}, u32[]{:S(2)}, u32[]{:S(2)}) collective-permute-start(f32[5,1,1024]{2,1,0:T(1,128)S(1)} %get-tuple-element.159), channel_id=1, source_target_pairs={{1,0},{2,1},{3,2},{4,3},{5,4},{6,5},{7,6},{8,7},{9,8},{10,9},{11,1... | collective-permute-start | bytes 61448 | tf_op jit(solution)/shard_map/ppermute | solution.py:26
  53.8 2.6 copy.184
  56.5 10.4 %gather_fusion = f32[1024,5,8]{2,1,0:T(8,128)} fusion(f32[5,8,1024]{1,0,2:T(8,128)} %copy.184, s32[1024]{0:T(1024)S(1)} %fusion.60), kind=kCustom, calls=%fused_computation.clone | custom fusion | bytes 331776 | tf_op jit(solution)/shard_map/jit(_take)/gather | solution.py:138
  66.9 2.7 copy.185
  69.6 10.4 %gather_fusion.1 = f32[1024,5,8]{2,1,0:T(8,128)} fusion(f32[5,8,1024]{1,0,2:T(8,128)} %copy.184, s32[1024]{0:T(1024)S(1)} %fusion.61), kind=kCustom, calls=%fused_computation.1.clone | custom fusion | bytes 331776 | tf_op jit(solution)/shard_map/jit(_take)/gather | solution.py:137
  79.9 2.6 copy.187
  82.5 10.4 %gather_fusion.2 = f32[1024,5,8]{2,1,0:T(8,128)} fusion(f32[5,8,1024]{1,0,2:T(8,128)} %copy.184, s32[1024]{0:T(1024)S(1)} %fusion.62), kind=kCustom, calls=%fused_computation.2.clone | custom fusion | bytes 331776 | tf_op jit(solution)/shard_map/jit(_take)/gather | solution.py:136
  92.9 2.6 copy.189
  95.6 10.4 %gather_fusion.3 = f32[1024,5,8]{2,1,0:T(8,128)} fusion(f32[5,8,1024]{1,0,2:T(8,128)} %copy.184, s32[1024]{0:T(1024)S(1)} %fusion.63), kind=kCustom, calls=%fused_computation.3.clone | custom fusion | bytes 331776 | tf_op jit(solution)/shard_map/jit(_take)/gather | solution.py:135
  106.0 2.6 copy.191
  109.2 169.2 %all-reduce.80.cloned.1.call-done = f32[3,65536]{1,0:T(4,128)} async-done(((f32[3,65536]{1,0:T(4,128)}), f32[3,65536]{1,0:T(4,128)}) %all-reduce.80.cloned.1.call-update) | async-done | bytes 786448 | tf_op jit(solution)/shard_map/psum | solution.py:114
  278.3 0.8 multiply_reduce_fusion.4
  279.1 11.6 %scatter_custom_fusion = f32[8192]{0:T(1024)S(1)} fusion(s32[2048]{0:T(1024)} %param.24, f32[2048]{0:T(1024)S(1)} %multiply_reduce_fusion.4, f32[]{:T(128)} %constant.59.clone.1), kind=kCustom, calls=%fused_computation.205 | custom fusion | flops 2048 | bytes 33280 | tf_op jit(solution)/shard_map/scatter-add | solution.py:119
  290.8 3.2 fusion.9
  294.2 2.7 copy.192
  296.8 10.4 %gather_fusion.4 = f32[1024,5,8]{2,1,0:T(8,128)} fusion(f32[5,8,1024]{1,0,2:T(8,128)} %copy.192, s32[1024]{0:T(1024)S(1)} %fusion.60), kind=kCustom, calls=%fused_computation.4.clone | custom fusion | bytes 331776 | tf_op jit(solution)/shard_map/jit(_take)/gather | solution.py:138
  307.2 10.3 %gather_fusion.5 = f32[1024,5,8]{2,1,0:T(8,128)} fusion(f32[5,8,1024]{1,0,2:T(8,128)} %copy.192, s32[1024]{0:T(1024)S(1)} %fusion.61), kind=kCustom, calls=%fused_computation.5.clone | custom fusion | bytes 331776 | tf_op jit(solution)/shard_map/jit(_take)/gather | solution.py:137
  317.5 10.4 %gather_fusion.6 = f32[1024,5,8]{2,1,0:T(8,128)} fusion(f32[5,8,1024]{1,0,2:T(8,128)} %copy.192, s32[1024]{0:T(1024)S(1)} %fusion.62), kind=kCustom, calls=%fused_computation.6.clone | custom fusion | bytes 331776 | tf_op jit(solution)/shard_map/jit(_take)/gather | solution.py:136
  327.9 10.4 %gather_fusion.7 = f32[1024,5,8]{2,1,0:T(8,128)} fusion(f32[5,8,1024]{1,0,2:T(8,128)} %copy.192, s32[1024]{0:T(1024)S(1)} %fusion.63), kind=kCustom, calls=%fused_computation.7.clone | custom fusion | bytes 331776 | tf_op jit(solution)/shard_map/jit(_take)/gather | solution.py:135
  338.3 2.6 copy.193
  340.9 2.6 copy.195
  343.5 2.6 copy.197
  346.2 2.6 copy.199
  349.1 4.1 collective-permute-start.3
  353.3 1.4 collective-permute-done.2
  355.0 37.8 %all-gather.8.cloned.1.call-done = f32[5,64,1024]{2,1,0:T(8,128)} async-done(((f32[5,8,1024]{2,1,0:T(8,128)}), f32[5,64,1024]{2,1,0:T(8,128)}) %all-gather.8.cloned.1.call-update) | async-done | bytes 1310736 | tf_op jit(solution)/shard_map/all_gather | solution.py:143
  392.8 3.2 fusion.7
  396.2 2.7 copy.200
  398.8 10.4 %gather_fusion.8 = f32[1024,5,8]{2,1,0:T(8,128)} fusion(f32[5,8,1024]{1,0,2:T(8,128)} %copy.200, s32[1024]{0:T(1024)S(1)} %fusion.60), kind=kCustom, calls=%fused_computation.8.clone | custom fusion | bytes 331776 | tf_op jit(solution)/shard_map/jit(_take)/gather | solution.py:138
  409.2 10.3 %gather_fusion.9 = f32[1024,5,8]{2,1,0:T(8,128)} fusion(f32[5,8,1024]{1,0,2:T(8,128)} %copy.200, s32[1024]{0:T(1024)S(1)} %fusion.61), kind=kCustom, calls=%fused_computation.9.clone | custom fusion | bytes 331776 | tf_op jit(solution)/shard_map/jit(_take)/gather | solution.py:137
  419.5 10.4 %gather_fusion.10 = f32[1024,5,8]{2,1,0:T(8,128)} fusion(f32[5,8,1024]{1,0,2:T(8,128)} %copy.200, s32[1024]{0:T(1024)S(1)} %fusion.62), kind=kCustom, calls=%fused_computation.10.clone | custom fusion | bytes 331776 | tf_op jit(solution)/shard_map/jit(_take)/gather | solution.py:136
  429.9 10.4 %gather_fusion.11 = f32[1024,5,8]{2,1,0:T(8,128)} fusion(f32[5,8,1024]{1,0,2:T(8,128)} %copy.200, s32[1024]{0:T(1024)S(1)} %fusion.63), kind=kCustom, calls=%fused_computation.11.clone | custom fusion | bytes 331776 | tf_op jit(solution)/shard_map/jit(_take)/gather | solution.py:135
  440.3 2.6 copy.201
  442.9 2.6 copy.203
  445.5 2.6 copy.205
  448.1 2.6 copy.207
  451.1 3.8 collective-permute-start.5
  455.0 1.5 collective-permute-done.4
  456.8 36.8 %all-gather.10.cloned.1.call-done = f32[5,64,1024]{2,1,0:T(8,128)} async-done(((f32[5,8,1024]{2,1,0:T(8,128)}), f32[5,64,1024]{2,1,0:T(8,128)}) %all-gather.10.cloned.1.call-update) | async-done | bytes 1310736 | tf_op jit(solution)/shard_map/all_gather | solution.py:143
  493.6 3.2 fusion.5
  496.8 0.9 fusion.14
  (89 shorter events, 5.6 us)
Async XLA Ops:
  7.4 270.9 %all-reduce.80.cloned.1.call-start = ((), (), s32[]{:S(2)}) async-start(), calls=%async_computation.1 | async-start | bytes 2097152 | tf_op jit(solution)/shard_map/psum | solution.py:114
  8.0 45.8 %copy-start.4 = (f32[5,1,8,1024]{3,2,1,0:T(8,128)S(1)}, f32[5,1,8,1024]{3,2,1,0:T(8,128)}, u32[]{:S(2)}) copy-start(f32[5,1,8,1024]{3,2,1,0:T(8,128)} %param.15) | copy-start | bytes 491524
  46.1 10.3 %copy-start.9 = (s32[4,1024]{1,0:T(4,128)S(1)}, s32[4,1024]{1,0:T(4,128)}, u32[]{:S(2)}) copy-start(s32[4,1024]{1,0:T(4,128)} %param.25) | copy-start | bytes 49156
  46.2 244.6 %all-gather.6.cloned.1.call-start = ((), (), s32[]{:S(2)}) async-start(), calls=%async_computation | async-start | bytes 1474560 | tf_op jit(solution)/shard_map/all_gather | solution.py:143
  47.3 61.6 %collective-permute-start = (f32[5,1,1024]{2,1,0:T(1,128)S(1)}, f32[5,1,1024]{2,1,0:T(1,128)S(1)}, u32[]{:S(2)}, u32[]{:S(2)}) collective-permute-start(f32[5,1,1024]{2,1,0:T(1,128)S(1)} %get-tuple-element.160), channel_id=1, source_target_pairs={{0,1},{1,2},{2,3},{3,4},{4,5},{5,6},{6,7},{7,8},{8,9},{9,10},{10,1... | collective-permute-start | bytes 61448 | tf_op jit(solution)/shard_map/ppermute | solution.py:24
  47.3 61.5 %collective-permute-start.1 = (f32[5,1,1024]{2,1,0:T(1,128)S(1)}, f32[5,1,1024]{2,1,0:T(1,128)S(1)}, u32[]{:S(2)}, u32[]{:S(2)}) collective-permute-start(f32[5,1,1024]{2,1,0:T(1,128)S(1)} %get-tuple-element.159), channel_id=1, source_target_pairs={{1,0},{2,1},{3,2},{4,3},{5,4},{6,5},{7,6},{8,7},{9,8},{10,9},{11,1... | collective-permute-start | bytes 61448 | tf_op jit(solution)/shard_map/ppermute | solution.py:26
  53.8 339.0 %all-gather.8.cloned.1.call-start = ((), (), s32[]{:S(2)}) async-start(), calls=%async_computation.2 | async-start | bytes 1474560 | tf_op jit(solution)/shard_map/all_gather | solution.py:143
  92.9 15.7 %copy-start.5 = (f32[1,8,1024]{2,1,0:T(8,128)S(1)}, f32[1,8,1024]{2,1,0:T(8,128)}, u32[]{:S(2)}) copy-start(f32[1,8,1024]{2,1,0:T(8,128)} %param.16) | copy-start | bytes 98308
  92.9 15.7 %copy-start.6 = (f32[3,1,8,1024]{3,2,1,0:T(8,128)S(1)}, f32[3,1,8,1024]{3,2,1,0:T(8,128)}, u32[]{:S(2)}) copy-start(f32[3,1,8,1024]{3,2,1,0:T(8,128)} %param.17) | copy-start | bytes 294916
  92.9 15.8 %copy-start.7 = (f32[1,8,1024]{2,1,0:T(8,128)S(1)}, f32[1,8,1024]{2,1,0:T(8,128)}, u32[]{:S(2)}) copy-start(f32[1,8,1024]{2,1,0:T(8,128)} %param.18) | copy-start | bytes 98308
  106.0 3.0 copy-start.10
  106.0 172.4 %copy-start.8 = (f32[3,2048]{1,0:T(4,128)S(1)}, f32[3,2048]{1,0:T(4,128)}, u32[]{:S(2)}) copy-start(f32[3,2048]{1,0:T(4,128)} %param.23) | copy-start | bytes 73732
  294.1 44.1 %copy-start.2 = (f32[5,8,1024]{2,1,0:T(8,128)}, f32[5,8,1024]{2,1,0:T(8,128)S(1)}, u32[]{:S(2)}) copy-start(f32[5,8,1024]{2,1,0:T(8,128)S(1)} %fusion.36) | copy-start | bytes 491524
  338.3 155.3 %all-gather.10.cloned.1.call-start = ((), (), s32[]{:S(2)}) async-start(), calls=%async_computation.3 | async-start | bytes 1474560 | tf_op jit(solution)/shard_map/all_gather | solution.py:143
  343.5 5.2 %copy-start.3 = (f32[5,8,1024]{2,1,0:T(8,128)S(1)}, f32[5,8,1024]{2,1,0:T(8,128)}, u32[]{:S(2)}) copy-start(f32[5,8,1024]{2,1,0:T(8,128)} %copy-done.2) | copy-start | bytes 491524
  348.8 5.8 %collective-permute-start.2 = (f32[5,1,1024]{2,1,0:T(1,128)S(1)}, f32[5,1,1024]{2,1,0:T(1,128)S(1)}, u32[]{:S(2)}, u32[]{:S(2)}) collective-permute-start(f32[5,1,1024]{2,1,0:T(1,128)S(1)} %get-tuple-element.148), channel_id=1, source_target_pairs={{0,1},{1,2},{2,3},{3,4},{4,5},{5,6},{6,7},{7,8},{8,9},{9,10},{10,1... | collective-permute-start | bytes 61448 | tf_op jit(solution)/shard_map/ppermute | solution.py:24
  349.1 5.6 %collective-permute-start.3 = (f32[5,1,1024]{2,1,0:T(1,128)S(1)}, f32[5,1,1024]{2,1,0:T(1,128)S(1)}, u32[]{:S(2)}, u32[]{:S(2)}) collective-permute-start(f32[5,1,1024]{2,1,0:T(1,128)S(1)} %get-tuple-element.147), channel_id=1, source_target_pairs={{1,0},{2,1},{3,2},{4,3},{5,4},{6,5},{7,6},{8,7},{9,8},{10,9},{11,1... | collective-permute-start | bytes 61448 | tf_op jit(solution)/shard_map/ppermute | solution.py:26
  396.2 44.1 %copy-start = (f32[5,8,1024]{2,1,0:T(8,128)}, f32[5,8,1024]{2,1,0:T(8,128)S(1)}, u32[]{:S(2)}) copy-start(f32[5,8,1024]{2,1,0:T(8,128)S(1)} %fusion.25) | copy-start | bytes 491524
  445.5 5.2 %copy-start.1 = (f32[5,8,1024]{2,1,0:T(8,128)S(1)}, f32[5,8,1024]{2,1,0:T(8,128)}, u32[]{:S(2)}) copy-start(f32[5,8,1024]{2,1,0:T(8,128)} %copy-done) | copy-start | bytes 491524
  450.8 5.7 %collective-permute-start.4 = (f32[5,1,1024]{2,1,0:T(1,128)S(1)}, f32[5,1,1024]{2,1,0:T(1,128)S(1)}, u32[]{:S(2)}, u32[]{:S(2)}) collective-permute-start(f32[5,1,1024]{2,1,0:T(1,128)S(1)} %get-tuple-element.137), channel_id=1, source_target_pairs={{0,1},{1,2},{2,3},{3,4},{4,5},{5,6},{6,7},{7,8},{8,9},{9,10},{10,1... | collective-permute-start | bytes 61448 | tf_op jit(solution)/shard_map/ppermute | solution.py:24
  451.1 5.4 %collective-permute-start.5 = (f32[5,1,1024]{2,1,0:T(1,128)S(1)}, f32[5,1,1024]{2,1,0:T(1,128)S(1)}, u32[]{:S(2)}, u32[]{:S(2)}) collective-permute-start(f32[5,1,1024]{2,1,0:T(1,128)S(1)} %get-tuple-element.136), channel_id=1, source_target_pairs={{1,0},{2,1},{3,2},{4,3},{5,4},{6,5},{7,6},{8,7},{9,8},{10,9},{11,1... | collective-permute-start | bytes 61448 | tf_op jit(solution)/shard_map/ppermute | solution.py:26
Sparse Core Ops, SparseCore 0:
  46.3 231.9 all-reduce.79
Sparse Core Ops, SparseCore 1:
  53.8 54.9 all-gather.5
  338.4 54.4 all-gather.7
  440.4 53.2 all-gather.9
where the time goes:
time: 506 us; the launch traced here: 505 us
  waiting for transfers between devices  247 us (49%)
  local copies, waits for them, and re-layouts  175 us (35%)
  other arithmetic  43.5 us (9%)
  between operations  15.5 us (3%)
  starting transfers between devices  15.1 us (3%)
  matrix products  9.46 us (2%)
    psum x1, waiting for transfers between devices, shards(): total = lax.psum(whole, 'space')  169 us
    all_gather x3, waiting for transfers between devices, shards(): every_instant = lax.all_gather(psi[:, None], 'inst', axis=1, tiled=True)  74.7 us
    gather x6, local copies, waits for them, and re-layouts, shards(): minus_y = jnp.take(psi, plane_nbr[1], axis=2)  39.1 us
    gather x6, local copies, waits for them, and re-layouts, shards(): plus_y = jnp.take(psi, plane_nbr[0], axis=2)  39 us
    gather x6, local copies, waits for them, and re-layouts, shards(): minus_z = jnp.take(psi, plane_nbr[3], axis=2)  38.9 us
    gather x6, local copies, waits for them, and re-layouts, shards(): plus_z = jnp.take(psi, plane_nbr[2], axis=2)  38.8 us
    div x4, other arithmetic, panel_block(): (observers[3][:, None] * jnp.cos(phase) + observers[4][:, None] * jnp.sin...  17.3 us
    ppermute x3, starting transfers between devices, padded_2(): lax.ppermute(head, axis, [((i + 1) % count, i) for i in range(count)])  14.3 us
  transfers between devices with their start and end apart: 10, of which 5 were waited for; matrix products, arithmetic and copies ran while one was open for 18% of the time, Pallas kernels for 0%

commit v1 on v0

--- a/solution.py
+++ b/solution.py
@@ -3,6 +3,7 @@
 import jax.numpy as jnp
 from jax import lax
 from jax.sharding import PartitionSpec as P
+from jax.lax import all_to_all, axis_size
 
 ITERS = 3
 GAMMA = 1.4
@@ -140,7 +141,9 @@
             (0.5 * (minus_a - plus_a), 0.5 * (minus_y - plus_y), 0.5 * (minus_z - plus_z))
         )[0]
         spread = 6.0 * psi - (minus_a + plus_a + plus_y + minus_y + plus_z + minus_z)
-        every_instant = lax.all_gather(psi[:, None], "inst", axis=1, tiled=True)
+        every_instant = jnp.concatenate(
+            all_to_all(jnp.stack(axis_size("inst") * [psi[:, None]], axis=0), "inst", 0, 0), axis=1
+        )
         others = jnp.arange(inst_count, dtype=jnp.int32)
         row_entry = spectral_coeff(
             jnp.mod(inst_id - others, inst_count).astype(jnp.float32), float(inst_count)

time: 506 us -> 477 us (0.943)
  waiting for transfers between devices: 247 us -> 200 us
  starting transfers between devices: 15.1 us -> 33.7 us
    all_gather x3 -> x0, waiting for transfers between devices: 74.7 us -> none  [shards(): every_instant = lax.all_gather(psi[:, None], 'inst', axis=1, tiled=True)]
    all_to_all x0 -> x3, waiting for transfers between devices: none -> 30.9 us  [shards(): all_to_all(jnp.stack(axis_size('inst') * [psi[:, None]], axis=0), 'inst',...]
    all_to_all x0 -> x3, starting transfers between devices: none -> 18.8 us  [shards(): all_to_all(jnp.stack(axis_size('inst') * [psi[:, None]], axis=0), 'inst',...]
  transfers between devices with their start and end apart: 10 -> 10, of which waited for: 5 -> 3; matrix products, arithmetic and copies ran while one was open for 18% -> 23% of each run, Pallas kernels for 0% -> 0%
where the time goes in v1:
time: 477 us; the launch traced here: 474 us
  waiting for transfers between devices  200 us (42%)
  local copies, waits for them, and re-layouts  178 us (37%)
  other arithmetic  43.5 us (9%)
  starting transfers between devices  33.7 us (7%)
  between operations  13.8 us (3%)
  matrix products  5.52 us (1%)
    psum x1, waiting for transfers between devices, shards(): total = lax.psum(whole, 'space')  169 us
    gather x6, local copies, waits for them, and re-layouts, shards(): plus_y = jnp.take(psi, plane_nbr[0], axis=2)  38.9 us
    gather x6, local copies, waits for them, and re-layouts, shards(): minus_z = jnp.take(psi, plane_nbr[3], axis=2)  38.9 us
    gather x6, local copies, waits for them, and re-layouts, shards(): plus_z = jnp.take(psi, plane_nbr[2], axis=2)  38.8 us
    gather x6, local copies, waits for them, and re-layouts, shards(): minus_y = jnp.take(psi, plane_nbr[1], axis=2)  38.8 us
    all_to_all x3, waiting for transfers between devices, shards(): all_to_all(jnp.stack(axis_size('inst') * [psi[:, None]], axis=0), 'inst',...  30.9 us
    all_to_all x3, starting transfers between devices, shards(): all_to_all(jnp.stack(axis_size('inst') * [psi[:, None]], axis=0), 'inst',...  18.8 us
    div x4, other arithmetic, panel_block(): (observers[3][:, None] * jnp.cos(phase) + observers[4][:, None] * jnp.sin...  17.3 us
  transfers between devices with their start and end apart: 10, of which 3 were waited for; matrix products, arithmetic and copies ran while one was open for 23% of the time, Pallas kernels for 0%

profile of v1, /device:TPU:2, one launch (start us, length us, event | category | flops | bytes accessed | tf_op | source)
XLA Modules:
  0.0 474.4 jit_solution(9735607217026168248)
XLA Ops:
  6.5 1.0 fusion.102
  7.7 6.4 %collective-permute-start.1 = (f32[5,1,1024]{2,1,0:T(1,128)S(1)}, f32[5,1,1024]{2,1,0:T(1,128)S(1)}, u32[]{:S(2)}, u32[]{:S(2)}) collective-permute-start(f32[5,1,1024]{2,1,0:T(1,128)S(1)} %get-tuple-element.159), channel_id=1, source_target_pairs={{1,0},{2,1},{3,2},{4,3},{5,4},{6,5},{7,6},{8,7},{9,8},{10,9},{11,1... | collective-permute-start | bytes 61448 | tf_op jit(solution)/shard_map/ppermute | solution.py:27
  14.7 38.1 %while.10 = (s32[]{:T(128)}, f32[4,3,16384]{2,1,0:T(4,128)}, f32[2,16]{1,0:T(2,128)}, f32[1,16]{1,0:T(1,128)S(1)}, f32[]{:T(128)}, /*index=5*/f32[4,3,16384]{2,1,0:T(4,128)}, f32[3,16]{1,0:T(4,128)}, s32[]{:T(128)}) while((s32[]{:T(128)}, f32[4,3,16384]{2,1,0:T(4,128)}, f32[2,16]{1,0:T(2,128)}, f32[1,16]{1,0:T(1,128)S(1)}, f32[]{:T(128)}, ...), condition=%wide.region_6.8_spmd, body=%wide.region_3.7_spmd.sunk | while | flops 6766594 | bytes 5637533 | solution.py:53
  14.7 1.0 dynamic-slice_bitcast_fusion.2
  15.7 1.2 fusion.107
  17.0 0.8 slice_bitcast_fusion.3
  17.7 4.3 fusion.108
  22.0 1.5 fusion.109
  24.3 1.0 dynamic-slice_bitcast_fusion.2
  25.3 1.2 fusion.107
  27.2 4.3 fusion.108
  31.6 1.5 fusion.109
  33.8 1.0 dynamic-slice_bitcast_fusion.2
  34.8 1.2 fusion.107
  36.8 4.3 fusion.108
  41.1 1.5 fusion.109
  43.3 1.0 dynamic-slice_bitcast_fusion.2
  44.3 1.2 fusion.107
  46.3 4.3 fusion.108
  50.6 1.5 fusion.109
  52.8 1.3 stack.9
  54.1 7.2 %all-to-all-start = ((f32[8,5,1,8,1024]{4,3,2,1,0:T(8,128)}), f32[8,5,1,8,1024]{4,3,2,1,0:T(8,128)S(1)}, u32[]{:S(2)}, u32[]{:S(2)}) async-start(f32[8,5,1,8,1024]{4,3,2,1,0:T(8,128)} %stack.9), calls=%async_computation | async-start | bytes 2621440 | tf_op jit(solution)/shard_map/all_to_all | solution.py:145
  61.3 2.6 copy.190
  64.0 10.3 %gather_fusion = f32[1024,5,8]{2,1,0:T(8,128)} fusion(f32[5,8,1024]{1,0,2:T(8,128)} %copy.190, s32[1024]{0:T(1024)S(1)} %fusion.60), kind=kCustom, calls=%fused_computation.clone | custom fusion | bytes 331776 | tf_op jit(solution)/shard_map/jit(_take)/gather | solution.py:139
  74.4 2.6 copy.191
  77.0 10.4 %gather_fusion.1 = f32[1024,5,8]{2,1,0:T(8,128)} fusion(f32[5,8,1024]{1,0,2:T(8,128)} %copy.190, s32[1024]{0:T(1024)S(1)} %fusion.61), kind=kCustom, calls=%fused_computation.1.clone | custom fusion | bytes 331776 | tf_op jit(solution)/shard_map/jit(_take)/gather | solution.py:138
  87.3 2.6 copy.193
  90.0 10.3 %gather_fusion.2 = f32[1024,5,8]{2,1,0:T(8,128)} fusion(f32[5,8,1024]{1,0,2:T(8,128)} %copy.190, s32[1024]{0:T(1024)S(1)} %fusion.62), kind=kCustom, calls=%fused_computation.2.clone | custom fusion | bytes 331776 | tf_op jit(solution)/shard_map/jit(_take)/gather | solution.py:137
  100.3 2.6 copy.195
  103.0 10.4 %gather_fusion.3 = f32[1024,5,8]{2,1,0:T(8,128)} fusion(f32[5,8,1024]{1,0,2:T(8,128)} %copy.190, s32[1024]{0:T(1024)S(1)} %fusion.63), kind=kCustom, calls=%fused_computation.3.clone | custom fusion | bytes 331776 | tf_op jit(solution)/shard_map/jit(_take)/gather | solution.py:136
  113.3 2.6 copy.197
  116.4 168.7 %all-reduce.80.cloned.1.call-done = f32[3,65536]{1,0:T(4,128)} async-done(((f32[3,65536]{1,0:T(4,128)}), f32[3,65536]{1,0:T(4,128)}) %all-reduce.80.cloned.1.call-update) | async-done | bytes 786448 | tf_op jit(solution)/shard_map/psum | solution.py:115
  285.1 0.8 multiply_reduce_fusion.4
  285.9 11.6 %scatter_custom_fusion = f32[8192]{0:T(1024)S(1)} fusion(s32[2048]{0:T(1024)} %param.24, f32[2048]{0:T(1024)S(1)} %multiply_reduce_fusion.4, f32[]{:T(128)} %constant.59.clone.1), kind=kCustom, calls=%fused_computation.205 | custom fusion | flops 2048 | bytes 33280 | tf_op jit(solution)/shard_map/scatter-add | solution.py:120
  297.5 1.8 fusion.9
  299.6 2.6 copy.198
  302.2 10.4 %gather_fusion.4 = f32[1024,5,8]{2,1,0:T(8,128)} fusion(f32[5,8,1024]{1,0,2:T(8,128)} %copy.198, s32[1024]{0:T(1024)S(1)} %fusion.60), kind=kCustom, calls=%fused_computation.4.clone | custom fusion | bytes 331776 | tf_op jit(solution)/shard_map/jit(_take)/gather | solution.py:139
  312.6 10.3 %gather_fusion.5 = f32[1024,5,8]{2,1,0:T(8,128)} fusion(f32[5,8,1024]{1,0,2:T(8,128)} %copy.198, s32[1024]{0:T(1024)S(1)} %fusion.61), kind=kCustom, calls=%fused_computation.5.clone | custom fusion | bytes 331776 | tf_op jit(solution)/shard_map/jit(_take)/gather | solution.py:138
  322.9 10.3 %gather_fusion.6 = f32[1024,5,8]{2,1,0:T(8,128)} fusion(f32[5,8,1024]{1,0,2:T(8,128)} %copy.198, s32[1024]{0:T(1024)S(1)} %fusion.62), kind=kCustom, calls=%fused_computation.6.clone | custom fusion | bytes 331776 | tf_op jit(solution)/shard_map/jit(_take)/gather | solution.py:137
  333.2 10.4 %gather_fusion.7 = f32[1024,5,8]{2,1,0:T(8,128)} fusion(f32[5,8,1024]{1,0,2:T(8,128)} %copy.198, s32[1024]{0:T(1024)S(1)} %fusion.63), kind=kCustom, calls=%fused_computation.7.clone | custom fusion | bytes 331776 | tf_op jit(solution)/shard_map/jit(_take)/gather | solution.py:136
  343.6 2.6 copy.199
  346.2 2.6 copy.201
  348.9 2.6 copy.203
  351.5 2.6 copy.205
  354.3 4.1 collective-permute-start.3
  358.4 1.2 stack.10
  359.6 7.0 %all-to-all-start.1 = ((f32[8,5,1,8,1024]{4,3,2,1,0:T(8,128)}), f32[8,5,1,8,1024]{4,3,2,1,0:T(8,128)S(1)}, u32[]{:S(2)}, u32[]{:S(2)}) async-start(f32[8,5,1,8,1024]{4,3,2,1,0:T(8,128)} %stack.10), calls=%async_computation.1 | async-start | bytes 2621440 | tf_op jit(solution)/shard_map/all_to_all | solution.py:145
  367.0 15.2 %all-to-all-done.1 = f32[8,5,1,8,1024]{4,3,2,1,0:T(8,128)S(1)} async-done(((f32[8,5,1,8,1024]{4,3,2,1,0:T(8,128)}), f32[8,5,1,8,1024]{4,3,2,1,0:T(8,128)S(1)}, u32[]{:S(2)}, u32[]{:S(2)}) %all-to-all-start.1) | async-done | bytes 1310752 | tf_op jit(solution)/shard_map/all_to_all | solution.py:145
  382.2 1.8 fusion.7
  384.2 2.6 copy.206
  386.8 10.4 %gather_fusion.8 = f32[1024,5,8]{2,1,0:T(8,128)} fusion(f32[5,8,1024]{1,0,2:T(8,128)} %copy.206, s32[1024]{0:T(1024)S(1)} %fusion.60), kind=kCustom, calls=%fused_computation.8.clone | custom fusion | bytes 331776 | tf_op jit(solution)/shard_map/jit(_take)/gather | solution.py:139
  397.2 10.3 %gather_fusion.9 = f32[1024,5,8]{2,1,0:T(8,128)} fusion(f32[5,8,1024]{1,0,2:T(8,128)} %copy.206, s32[1024]{0:T(1024)S(1)} %fusion.61), kind=kCustom, calls=%fused_computation.9.clone | custom fusion | bytes 331776 | tf_op jit(solution)/shard_map/jit(_take)/gather | solution.py:138
  407.5 10.3 %gather_fusion.10 = f32[1024,5,8]{2,1,0:T(8,128)} fusion(f32[5,8,1024]{1,0,2:T(8,128)} %copy.206, s32[1024]{0:T(1024)S(1)} %fusion.62), kind=kCustom, calls=%fused_computation.10.clone | custom fusion | bytes 331776 | tf_op jit(solution)/shard_map/jit(_take)/gather | solution.py:137
  417.8 10.4 %gather_fusion.11 = f32[1024,5,8]{2,1,0:T(8,128)} fusion(f32[5,8,1024]{1,0,2:T(8,128)} %copy.206, s32[1024]{0:T(1024)S(1)} %fusion.63), kind=kCustom, calls=%fused_computation.11.clone | custom fusion | bytes 331776 | tf_op jit(solution)/shard_map/jit(_take)/gather | solution.py:136
  428.3 2.6 copy.207
  430.9 2.6 copy.209
  433.5 2.6 copy.211
  436.1 2.6 copy.213
  439.0 3.8 collective-permute-start.5
  442.9 1.2 stack.11
  444.1 4.6 all-to-all-start.2
  449.1 15.7 %all-to-all-done.2 = f32[8,5,1,8,1024]{4,3,2,1,0:T(8,128)S(1)} async-done(((f32[8,5,1,8,1024]{4,3,2,1,0:T(8,128)}), f32[8,5,1,8,1024]{4,3,2,1,0:T(8,128)S(1)}, u32[]{:S(2)}, u32[]{:S(2)}) %all-to-all-start.2) | async-done | bytes 1310752 | tf_op jit(solution)/shard_map/all_to_all | solution.py:145
  464.8 1.8 fusion.5
  466.7 0.9 fusion.14
  (81 shorter events, 8.4 us)
Async XLA Ops:
  6.5 278.6 %all-reduce.80.cloned.1.call-start = ((), (), s32[]{:S(2)}) async-start(), calls=%async_computation.3 | async-start | bytes 2097152 | tf_op jit(solution)/shard_map/psum | solution.py:115
  7.6 108.5 %collective-permute-start = (f32[5,1,1024]{2,1,0:T(1,128)S(1)}, f32[5,1,1024]{2,1,0:T(1,128)S(1)}, u32[]{:S(2)}, u32[]{:S(2)}) collective-permute-start(f32[5,1,1024]{2,1,0:T(1,128)S(1)} %get-tuple-element.160), channel_id=1, source_target_pairs={{0,1},{1,2},{2,3},{3,4},{4,5},{5,6},{6,7},{7,8},{8,9},{9,10},{10,1... | collective-permute-start | bytes 61448 | tf_op jit(solution)/shard_map/ppermute | solution.py:25
  7.7 108.4 %collective-permute-start.1 = (f32[5,1,1024]{2,1,0:T(1,128)S(1)}, f32[5,1,1024]{2,1,0:T(1,128)S(1)}, u32[]{:S(2)}, u32[]{:S(2)}) collective-permute-start(f32[5,1,1024]{2,1,0:T(1,128)S(1)} %get-tuple-element.159), channel_id=1, source_target_pairs={{1,0},{2,1},{3,2},{4,3},{5,4},{6,5},{7,6},{8,7},{9,8},{10,9},{11,1... | collective-permute-start | bytes 61448 | tf_op jit(solution)/shard_map/ppermute | solution.py:27
  14.7 38.1 %copy-start = (f32[5,1,8,1024]{3,2,1,0:T(8,128)S(1)}, f32[5,1,8,1024]{3,2,1,0:T(8,128)}, u32[]{:S(2)}) copy-start(f32[5,1,8,1024]{3,2,1,0:T(8,128)} %param.15) | copy-start | bytes 491524
  52.8 11.1 %copy-start.5 = (s32[4,1024]{1,0:T(4,128)S(1)}, s32[4,1024]{1,0:T(4,128)}, u32[]{:S(2)}) copy-start(s32[4,1024]{1,0:T(4,128)} %param.25) | copy-start | bytes 49156
  54.1 243.4 %all-to-all-start = ((f32[8,5,1,8,1024]{4,3,2,1,0:T(8,128)}), f32[8,5,1,8,1024]{4,3,2,1,0:T(8,128)S(1)}, u32[]{:S(2)}, u32[]{:S(2)}) async-start(f32[8,5,1,8,1024]{4,3,2,1,0:T(8,128)} %stack.9), calls=%async_computation | async-start | bytes 2621440 | tf_op jit(solution)/shard_map/all_to_all | solution.py:145
  74.3 15.6 %copy-start.1 = (f32[1,8,1024]{2,1,0:T(8,128)S(1)}, f32[1,8,1024]{2,1,0:T(8,128)}, u32[]{:S(2)}) copy-start(f32[1,8,1024]{2,1,0:T(8,128)} %param.16) | copy-start | bytes 98308
  74.4 15.6 %copy-start.2 = (f32[3,1,8,1024]{3,2,1,0:T(8,128)S(1)}, f32[3,1,8,1024]{3,2,1,0:T(8,128)}, u32[]{:S(2)}) copy-start(f32[3,1,8,1024]{3,2,1,0:T(8,128)} %param.17) | copy-start | bytes 294916
  100.3 15.6 %copy-start.3 = (f32[1,8,1024]{2,1,0:T(8,128)S(1)}, f32[1,8,1024]{2,1,0:T(8,128)}, u32[]{:S(2)}) copy-start(f32[1,8,1024]{2,1,0:T(8,128)} %param.18) | copy-start | bytes 98308
  103.0 13.3 %copy-start.6 = (pred[3]{0:T(512)(128)(4,1)S(1)}, pred[3]{0:T(512)(128)(4,1)}, u32[]{:S(2)}) copy-start(pred[3]{0:T(512)(128)(4,1)} %constant.63.clone.1) | copy-start | bytes 13
  113.3 171.8 %copy-start.4 = (f32[3,2048]{1,0:T(4,128)S(1)}, f32[3,2048]{1,0:T(4,128)}, u32[]{:S(2)}) copy-start(f32[3,2048]{1,0:T(4,128)} %param.23) | copy-start | bytes 73732
  354.1 12.6 %collective-permute-start.2 = (f32[5,1,1024]{2,1,0:T(1,128)S(1)}, f32[5,1,1024]{2,1,0:T(1,128)S(1)}, u32[]{:S(2)}, u32[]{:S(2)}) collective-permute-start(f32[5,1,1024]{2,1,0:T(1,128)S(1)} %get-tuple-element.148), channel_id=1, source_target_pairs={{0,1},{1,2},{2,3},{3,4},{4,5},{5,6},{6,7},{7,8},{8,9},{9,10},{10,1... | collective-permute-start | bytes 61448 | tf_op jit(solution)/shard_map/ppermute | solution.py:25
  354.3 12.3 %collective-permute-start.3 = (f32[5,1,1024]{2,1,0:T(1,128)S(1)}, f32[5,1,1024]{2,1,0:T(1,128)S(1)}, u32[]{:S(2)}, u32[]{:S(2)}) collective-permute-start(f32[5,1,1024]{2,1,0:T(1,128)S(1)} %get-tuple-element.147), channel_id=1, source_target_pairs={{1,0},{2,1},{3,2},{4,3},{5,4},{6,5},{7,6},{8,7},{9,8},{10,9},{11,1... | collective-permute-start | bytes 61448 | tf_op jit(solution)/shard_map/ppermute | solution.py:27
  359.6 22.5 %all-to-all-start.1 = ((f32[8,5,1,8,1024]{4,3,2,1,0:T(8,128)}), f32[8,5,1,8,1024]{4,3,2,1,0:T(8,128)S(1)}, u32[]{:S(2)}, u32[]{:S(2)}) async-start(f32[8,5,1,8,1024]{4,3,2,1,0:T(8,128)} %stack.10), calls=%async_computation.1 | async-start | bytes 2621440 | tf_op jit(solution)/shard_map/all_to_all | solution.py:145
  438.7 10.1 %collective-permute-start.4 = (f32[5,1,1024]{2,1,0:T(1,128)S(1)}, f32[5,1,1024]{2,1,0:T(1,128)S(1)}, u32[]{:S(2)}, u32[]{:S(2)}) collective-permute-start(f32[5,1,1024]{2,1,0:T(1,128)S(1)} %get-tuple-element.137), channel_id=1, source_target_pairs={{0,1},{1,2},{2,3},{3,4},{4,5},{5,6},{6,7},{7,8},{8,9},{9,10},{10,1... | collective-permute-start | bytes 61448 | tf_op jit(solution)/shard_map/ppermute | solution.py:25
  439.0 9.8 %collective-permute-start.5 = (f32[5,1,1024]{2,1,0:T(1,128)S(1)}, f32[5,1,1024]{2,1,0:T(1,128)S(1)}, u32[]{:S(2)}, u32[]{:S(2)}) collective-permute-start(f32[5,1,1024]{2,1,0:T(1,128)S(1)} %get-tuple-element.136), channel_id=1, source_target_pairs={{1,0},{2,1},{3,2},{4,3},{5,4},{6,5},{7,6},{8,7},{9,8},{10,9},{11,1... | collective-permute-start | bytes 61448 | tf_op jit(solution)/shard_map/ppermute | solution.py:27
  444.1 20.7 %all-to-all-start.2 = ((f32[8,5,1,8,1024]{4,3,2,1,0:T(8,128)}), f32[8,5,1,8,1024]{4,3,2,1,0:T(8,128)S(1)}, u32[]{:S(2)}, u32[]{:S(2)}) async-start(f32[8,5,1,8,1024]{4,3,2,1,0:T(8,128)} %stack.11), calls=%async_computation.2 | async-start | bytes 2621440 | tf_op jit(solution)/shard_map/all_to_all | solution.py:145
Sparse Core Ops, SparseCore 0:
  52.9 232.1 all-reduce.79
